TPU v7x, 512 devices: a whole 4x4x16 slice. The times are simulated.
512 devices in a mesh: tm: 64 (over y, z), state: 8 (over x, core).
Axes of the slice: x: 4, y: 4, z: 16, core: 2. Of those that a mesh axis runs over, the one named last changes fastest.
Arguments:
- obs: int32 [512], P('tm'), may hold values from 0 to 255
- emit_logits: float32 [256, 2048], P(None, 'state'), may hold values from -0.6 to 0.6
- trans_logits: float32 [16, 3, 128, 128], P('state'), may hold values from -5 to 17
- band_cols: int32 [16, 3], replicated, may hold values from 0 to 15, as said below
- init_logits: float32 [2048], replicated, may hold values from -6 to 6
Outputs:
- posterior: float32 [64, 2048], P('tm', 'state')
Inputs may be any that keep to these rules, and one draw needn't show every extreme that they name: Row r of band_cols names 3 different block columns, the first of them r itself.
All inputs are finite; a program needn't handle non-finite values.
Results may differ from a plain program's by a relative error of at most 0.0006.
The roundings to bfloat16 on the way count: a program that leaves them out, or rounds other values in their place, can miss the bound.
Values may be sent and summed in bfloat16 or wider, within the bound.
A program may use at most 64 MiB of HBM per device.

v0:
```python
import jax
import jax.numpy as jnp
from jax import lax
from jax.sharding import PartitionSpec as P

SEQS = 1


SMOOTH = 0.001


def from_behind(value, axis, steps):
    count = lax.axis_size(axis)
    initial, last = (max(0, -steps), min(count, count - steps))
    return lax.ppermute(value, axis, [(source, source + steps) for source in range(initial, last)])


def form_columns(emit_full, blocks, band_cols, first_col, col_count):
    states = emit_full.shape[1]
    block_count = blocks.shape[0]
    block_size = blocks.shape[2]
    state_rows = jnp.arange(states)[:, None]
    state_cols = first_col + jnp.arange(col_count)[None, :]
    matrix = (state_rows == state_cols).astype(jnp.float32)
    col_scale = jnp.zeros((col_count,), jnp.float32)
    for moment in range(emit_full.shape[0] - 1, -1, -1):
        scaled = (jnp.exp(emit_full[moment])[:, None] * matrix).astype(jnp.bfloat16)
        picked = scaled.reshape(block_count, block_size, col_count)[band_cols]
        product = jnp.einsum(
            "rkij,rkjc->ric", blocks, picked, preferred_element_type=jnp.float32
        ).reshape(states, col_count)
        matrix = product + SMOOTH / states * jnp.sum(scaled, axis=0, dtype=jnp.float32)[None, :]
        col_peak = jnp.max(matrix, axis=0)
        matrix = matrix / col_peak[None, :]
        col_scale = col_scale + jnp.log(col_peak)
    return jnp.log(matrix) + col_scale[None, :]


def on_device(obs, emit_logits, trans_logits, band_cols, init_logits):
    col_count = emit_logits.shape[1]
    state_index = lax.axis_index("state")
    first_col = state_index * col_count
    groups = lax.axis_size("tm") // SEQS
    position = lax.axis_index("tm") % groups
    blocks_own = ((1.0 - SMOOTH) * jax.nn.softmax(trans_logits, axis=(1, 3))).astype(jnp.bfloat16)
    blocks = lax.all_gather(blocks_own, "state", axis=0, tiled=True)
    log_emit = jax.nn.log_softmax(emit_logits, axis=0)
    symbols = emit_logits.shape[0]
    onehot = (obs[:, None] == jnp.arange(symbols)[None, :]).astype(jnp.float32)
    emit_own = jnp.dot(onehot, log_emit, precision=lax.Precision.HIGHEST)
    emit_full = lax.all_gather(emit_own, "state", axis=1, tiled=True)
    own_log = form_columns(emit_full, blocks, band_cols, first_col, col_count)
    left_log = from_behind(own_log, "tm", 1)
    row_peak = lax.pmax(jnp.max(own_log, axis=1), "state")
    peak_own = lax.dynamic_slice_in_dim(row_peak, first_col, col_count)
    shifted = left_log + peak_own[None, :]
    left_peak = lax.pmax(jnp.max(shifted, axis=1), "state")
    weights = jnp.exp(shifted - left_peak[:, None]).astype(jnp.bfloat16)
    right_exp = jnp.exp(own_log - row_peak[:, None]).astype(jnp.bfloat16)
    prior_log = jax.nn.log_softmax(init_logits)
    summed = jnp.dot(
        lax.all_gather(weights, "state", axis=1, tiled=True),
        right_exp,
        preferred_element_type=jnp.float32,
    )
    pair_log = left_peak[:, None] + jnp.log(summed)
    chosen = jnp.where(position == 0, own_log, pair_log)
    col_max = jnp.max(chosen, axis=0)
    scaled_exp = jnp.exp(chosen - col_max[None, :])

    def apply_cols(vector):
        vector_top = jnp.max(vector)
        mixture = jnp.dot(
            jnp.exp(vector - vector_top)[None, :], scaled_exp, precision=lax.Precision.HIGHEST
        )[0]
        return vector_top + col_max + jnp.log(mixture)

    start_cols = apply_cols(prior_log)

    def advance(counter, current):
        incoming = from_behind(current, "tm", 2)
        whole_vector = lax.all_gather(incoming, "state", axis=0, tiled=True)
        return jnp.where(position < 2, start_cols, apply_cols(whole_vector))

    alpha_cols = lax.fori_loop(0, groups // 2 - 1, advance, start_cols)
    vector_top = lax.pmax(jnp.max(alpha_cols), "state")
    total_sum = lax.psum(jnp.sum(jnp.exp(alpha_cols - vector_top)), "state")
    posterior = alpha_cols - vector_top - jnp.log(total_sum)
    return posterior[None, :]


def solution(mesh):
    return jax.shard_map(
        on_device,
        mesh=mesh,
        in_specs=(P("tm"), P(None, "state"), P("state", None, None, None), P(), P()),
        out_specs=P("tm", "state"),
        check_vma=False,
    )
```

profile of v0, /device:TPU:25, one launch (start us, length us, event | category | flops | bytes accessed | tf_op | source)
XLA Modules:
  0.0 896.1 jit_solution(222817929016838769)
XLA Ops:
  13.3 13.6 %all_gather.15 = f32[8,2048]{1,0:T(8,128)S(1)} all-gather(f32[8,256]{1,0:T(8,128)S(1)} %fusion.15), channel_id=1, replica_groups=mesh['tm'=64,'state'=8] {'state'}, dimensions={1}, use_global_device_ids=true | all-gather | bytes 73728 | tf_op jit(solution)/shard_map/all_gather | solution.py:51
  30.6 17.1 %all-gather.6.cloned.1.call-done = bf16[16,3,128,128]{3,2,1,0:T(8,128)(2,1)} async-done(((bf16[2,3,128,128]{3,2,1,0:T(8,128)(2,1)}), bf16[16,3,128,128]{3,2,1,0:T(8,128)(2,1)}) %all-gather.6.cloned.1.call-update) | async-done | bytes 1572880 | tf_op jit(solution)/shard_map/all_gather | solution.py:46
  98.4 12.8 %pmax.21 = f32[2048]{0:T(1024)S(1)} all-reduce(f32[2048]{0:T(1024)S(1)} %bitcast.156), channel_id=1, replica_groups=mesh['tm'=64,'state'=8] {'state'}, use_global_device_ids=true, to_apply=%region_24.25 | all-reduce | flops 2048 | bytes 16384 | tf_op jit(solution)/shard_map/pmax | solution.py:54
  111.3 33.6 %collective-permute-done.1 = f32[2048,256]{1,0:T(8,128)S(1)} collective-permute-done((f32[2048,256]{1,0:T(8,128)}, f32[2048,256]{1,0:T(8,128)S(1)}, u32[]{:S(2)}, u32[]{:S(2)}) %collective-permute-start.1) | collective-permute-done | bytes 2097184 | tf_op jit(solution)/shard_map/ppermute | solution.py:15
  145.3 12.8 %pmax.22 = f32[2048]{0:T(1024)S(1)} all-reduce(f32[2048]{0:T(1024)S(1)} %add_reduce_fusion.1), channel_id=1, replica_groups=mesh['tm'=64,'state'=8] {'state'}, use_global_device_ids=true, to_apply=%region_26.27 | all-reduce | flops 2048 | bytes 16384 | tf_op jit(solution)/shard_map/pmax | solution.py:57
  164.7 54.5 %all-gather.8.cloned.1.call-done = bf16[2048,2048]{1,0:T(8,128)(2,1)} async-done(((bf16[2048,256]{1,0:T(8,128)(2,1)}), bf16[2048,2048]{1,0:T(8,128)(2,1)}) %all-gather.8.cloned.1.call-update) | async-done | bytes 8388624 | tf_op jit(solution)/shard_map/all_gather | solution.py:62
  228.5 630.9 %while.12 = (s32[]{:T(128)}, f32[256]{0:T(256)S(1)}, pred[]{:T(512)}, f32[256]{0:T(256)S(1)}, f32[2048,256]{1,0:T(8,128)S(1)}, /*index=5*/f32[256]{0:T(256)S(1)}, s32[]{:T(128)}, f32[]{:T(128)}) while((s32[]{:T(128)}, f32[256]{0:T(256)S(1)}, pred[]{:T(512)}, f32[256]{0:T(256)S(1)}, f32[2048,256]{1,0:T(8,128)S(1)}, ...), condition=%wide.region_30.31_spmd, body=%wide.region_28.30_spmd.sunk | while | flops 6296321 | bytes 2148494 | solution.py:85
  236.3 10.8 %all-gather.2 = f32[8,1,256]{2,1,0:T(1,128)S(1)} all-gather(f32[1,1,256]{2,1,0:T(1,128)S(1)} %bitcast.157), channel_id=1, replica_groups=mesh['tm'=64,'state'=8] {'state'}, dimensions={0}, use_global_device_ids=true | all-gather | bytes 9216 | tf_op jit(solution)/shard_map/while/body/eval_jaxpr/all_gather | solution.py:82
  257.4 9.0 %all-gather.2 = f32[8,1,256]{2,1,0:T(1,128)S(1)} all-gather(f32[1,1,256]{2,1,0:T(1,128)S(1)} %bitcast.157), channel_id=1, replica_groups=mesh['tm'=64,'state'=8] {'state'}, dimensions={0}, use_global_device_ids=true | all-gather | bytes 9216 | tf_op jit(solution)/shard_map/while/body/eval_jaxpr/all_gather | solution.py:82
  276.7 10.9 %all-gather.2 = f32[8,1,256]{2,1,0:T(1,128)S(1)} all-gather(f32[1,1,256]{2,1,0:T(1,128)S(1)} %bitcast.157), channel_id=1, replica_groups=mesh['tm'=64,'state'=8] {'state'}, dimensions={0}, use_global_device_ids=true | all-gather | bytes 9216 | tf_op jit(solution)/shard_map/while/body/eval_jaxpr/all_gather | solution.py:82
  298.0 9.0 %all-gather.2 = f32[8,1,256]{2,1,0:T(1,128)S(1)} all-gather(f32[1,1,256]{2,1,0:T(1,128)S(1)} %bitcast.157), channel_id=1, replica_groups=mesh['tm'=64,'state'=8] {'state'}, dimensions={0}, use_global_device_ids=true | all-gather | bytes 9216 | tf_op jit(solution)/shard_map/while/body/eval_jaxpr/all_gather | solution.py:82
  317.4 10.9 %all-gather.2 = f32[8,1,256]{2,1,0:T(1,128)S(1)} all-gather(f32[1,1,256]{2,1,0:T(1,128)S(1)} %bitcast.157), channel_id=1, replica_groups=mesh['tm'=64,'state'=8] {'state'}, dimensions={0}, use_global_device_ids=true | all-gather | bytes 9216 | tf_op jit(solution)/shard_map/while/body/eval_jaxpr/all_gather | solution.py:82
  338.6 9.0 %all-gather.2 = f32[8,1,256]{2,1,0:T(1,128)S(1)} all-gather(f32[1,1,256]{2,1,0:T(1,128)S(1)} %bitcast.157), channel_id=1, replica_groups=mesh['tm'=64,'state'=8] {'state'}, dimensions={0}, use_global_device_ids=true | all-gather | bytes 9216 | tf_op jit(solution)/shard_map/while/body/eval_jaxpr/all_gather | solution.py:82
  358.0 10.9 %all-gather.2 = f32[8,1,256]{2,1,0:T(1,128)S(1)} all-gather(f32[1,1,256]{2,1,0:T(1,128)S(1)} %bitcast.157), channel_id=1, replica_groups=mesh['tm'=64,'state'=8] {'state'}, dimensions={0}, use_global_device_ids=true | all-gather | bytes 9216 | tf_op jit(solution)/shard_map/while/body/eval_jaxpr/all_gather | solution.py:82
  379.3 9.0 %all-gather.2 = f32[8,1,256]{2,1,0:T(1,128)S(1)} all-gather(f32[1,1,256]{2,1,0:T(1,128)S(1)} %bitcast.157), channel_id=1, replica_groups=mesh['tm'=64,'state'=8] {'state'}, dimensions={0}, use_global_device_ids=true | all-gather | bytes 9216 | tf_op jit(solution)/shard_map/while/body/eval_jaxpr/all_gather | solution.py:82
  398.6 10.9 %all-gather.2 = f32[8,1,256]{2,1,0:T(1,128)S(1)} all-gather(f32[1,1,256]{2,1,0:T(1,128)S(1)} %bitcast.157), channel_id=1, replica_groups=mesh['tm'=64,'state'=8] {'state'}, dimensions={0}, use_global_device_ids=true | all-gather | bytes 9216 | tf_op jit(solution)/shard_map/while/body/eval_jaxpr/all_gather | solution.py:82
  419.9 9.0 %all-gather.2 = f32[8,1,256]{2,1,0:T(1,128)S(1)} all-gather(f32[1,1,256]{2,1,0:T(1,128)S(1)} %bitcast.157), channel_id=1, replica_groups=mesh['tm'=64,'state'=8] {'state'}, dimensions={0}, use_global_device_ids=true | all-gather | bytes 9216 | tf_op jit(solution)/shard_map/while/body/eval_jaxpr/all_gather | solution.py:82
  439.2 10.9 %all-gather.2 = f32[8,1,256]{2,1,0:T(1,128)S(1)} all-gather(f32[1,1,256]{2,1,0:T(1,128)S(1)} %bitcast.157), channel_id=1, replica_groups=mesh['tm'=64,'state'=8] {'state'}, dimensions={0}, use_global_device_ids=true | all-gather | bytes 9216 | tf_op jit(solution)/shard_map/while/body/eval_jaxpr/all_gather | solution.py:82
  460.5 9.0 %all-gather.2 = f32[8,1,256]{2,1,0:T(1,128)S(1)} all-gather(f32[1,1,256]{2,1,0:T(1,128)S(1)} %bitcast.157), channel_id=1, replica_groups=mesh['tm'=64,'state'=8] {'state'}, dimensions={0}, use_global_device_ids=true | all-gather | bytes 9216 | tf_op jit(solution)/shard_map/while/body/eval_jaxpr/all_gather | solution.py:82
  479.9 10.9 %all-gather.2 = f32[8,1,256]{2,1,0:T(1,128)S(1)} all-gather(f32[1,1,256]{2,1,0:T(1,128)S(1)} %bitcast.157), channel_id=1, replica_groups=mesh['tm'=64,'state'=8] {'state'}, dimensions={0}, use_global_device_ids=true | all-gather | bytes 9216 | tf_op jit(solution)/shard_map/while/body/eval_jaxpr/all_gather | solution.py:82
  501.1 9.0 %all-gather.2 = f32[8,1,256]{2,1,0:T(1,128)S(1)} all-gather(f32[1,1,256]{2,1,0:T(1,128)S(1)} %bitcast.157), channel_id=1, replica_groups=mesh['tm'=64,'state'=8] {'state'}, dimensions={0}, use_global_device_ids=true | all-gather | bytes 9216 | tf_op jit(solution)/shard_map/while/body/eval_jaxpr/all_gather | solution.py:82
  520.5 10.9 %all-gather.2 = f32[8,1,256]{2,1,0:T(1,128)S(1)} all-gather(f32[1,1,256]{2,1,0:T(1,128)S(1)} %bitcast.157), channel_id=1, replica_groups=mesh['tm'=64,'state'=8] {'state'}, dimensions={0}, use_global_device_ids=true | all-gather | bytes 9216 | tf_op jit(solution)/shard_map/while/body/eval_jaxpr/all_gather | solution.py:82
  561.1 10.9 %all-gather.2 = f32[8,1,256]{2,1,0:T(1,128)S(1)} all-gather(f32[1,1,256]{2,1,0:T(1,128)S(1)} %bitcast.157), channel_id=1, replica_groups=mesh['tm'=64,'state'=8] {'state'}, dimensions={0}, use_global_device_ids=true | all-gather | bytes 9216 | tf_op jit(solution)/shard_map/while/body/eval_jaxpr/all_gather | solution.py:82
  601.7 10.9 %all-gather.2 = f32[8,1,256]{2,1,0:T(1,128)S(1)} all-gather(f32[1,1,256]{2,1,0:T(1,128)S(1)} %bitcast.157), channel_id=1, replica_groups=mesh['tm'=64,'state'=8] {'state'}, dimensions={0}, use_global_device_ids=true | all-gather | bytes 9216 | tf_op jit(solution)/shard_map/while/body/eval_jaxpr/all_gather | solution.py:82
  642.4 10.9 %all-gather.2 = f32[8,1,256]{2,1,0:T(1,128)S(1)} all-gather(f32[1,1,256]{2,1,0:T(1,128)S(1)} %bitcast.157), channel_id=1, replica_groups=mesh['tm'=64,'state'=8] {'state'}, dimensions={0}, use_global_device_ids=true | all-gather | bytes 9216 | tf_op jit(solution)/shard_map/while/body/eval_jaxpr/all_gather | solution.py:82
  683.0 10.9 %all-gather.2 = f32[8,1,256]{2,1,0:T(1,128)S(1)} all-gather(f32[1,1,256]{2,1,0:T(1,128)S(1)} %bitcast.157), channel_id=1, replica_groups=mesh['tm'=64,'state'=8] {'state'}, dimensions={0}, use_global_device_ids=true | all-gather | bytes 9216 | tf_op jit(solution)/shard_map/while/body/eval_jaxpr/all_gather | solution.py:82
  723.6 10.9 %all-gather.2 = f32[8,1,256]{2,1,0:T(1,128)S(1)} all-gather(f32[1,1,256]{2,1,0:T(1,128)S(1)} %bitcast.157), channel_id=1, replica_groups=mesh['tm'=64,'state'=8] {'state'}, dimensions={0}, use_global_device_ids=true | all-gather | bytes 9216 | tf_op jit(solution)/shard_map/while/body/eval_jaxpr/all_gather | solution.py:82
  764.2 10.9 %all-gather.2 = f32[8,1,256]{2,1,0:T(1,128)S(1)} all-gather(f32[1,1,256]{2,1,0:T(1,128)S(1)} %bitcast.157), channel_id=1, replica_groups=mesh['tm'=64,'state'=8] {'state'}, dimensions={0}, use_global_device_ids=true | all-gather | bytes 9216 | tf_op jit(solution)/shard_map/while/body/eval_jaxpr/all_gather | solution.py:82
  804.9 10.9 %all-gather.2 = f32[8,1,256]{2,1,0:T(1,128)S(1)} all-gather(f32[1,1,256]{2,1,0:T(1,128)S(1)} %bitcast.157), channel_id=1, replica_groups=mesh['tm'=64,'state'=8] {'state'}, dimensions={0}, use_global_device_ids=true | all-gather | bytes 9216 | tf_op jit(solution)/shard_map/while/body/eval_jaxpr/all_gather | solution.py:82
  845.5 10.9 %all-gather.2 = f32[8,1,256]{2,1,0:T(1,128)S(1)} all-gather(f32[1,1,256]{2,1,0:T(1,128)S(1)} %bitcast.157), channel_id=1, replica_groups=mesh['tm'=64,'state'=8] {'state'}, dimensions={0}, use_global_device_ids=true | all-gather | bytes 9216 | tf_op jit(solution)/shard_map/while/body/eval_jaxpr/all_gather | solution.py:82
  860.0 12.7 %pmax.23 = f32[]{:T(128)} all-reduce(f32[]{:T(128)} %reduce_max.175), channel_id=1, replica_groups=mesh['tm'=64,'state'=8] {'state'}, use_global_device_ids=true, to_apply=%region_32.33 | all-reduce | flops 1 | bytes 8 | tf_op jit(solution)/shard_map/pmax | solution.py:86
  874.0 13.3 %psum.7 = f32[]{:T(128)} all-reduce(f32[]{:T(128)} %exponential_reduce_fusion.2), channel_id=1, replica_groups=mesh['tm'=64,'state'=8] {'state'}, use_global_device_ids=true, to_apply=%region_34.35 | all-reduce | flops 1 | bytes 8 | tf_op jit(solution)/shard_map/psum | solution.py:87
  (276 shorter events, 472.2 us)
Async XLA Ops:
  6.5 41.2 %all-gather.6.cloned.1.call-start = ((), (), s32[]{:S(2)}) async-start(), calls=%async_computation | async-start | bytes 1769472 | tf_op jit(solution)/shard_map/all_gather | solution.py:46
  10.8 208.4 %all-gather.8.cloned.1.call-start = ((), (), s32[]{:S(2)}) async-start(), calls=%async_computation.1 | async-start | bytes 9437184 | tf_op jit(solution)/shard_map/all_gather | solution.py:62
  92.9 52.0 %collective-permute-start.1 = (f32[2048,256]{1,0:T(8,128)}, f32[2048,256]{1,0:T(8,128)S(1)}, u32[]{:S(2)}, u32[]{:S(2)}) collective-permute-start(f32[2048,256]{1,0:T(8,128)} %fusion.4), channel_id=1, source_target_pairs={{0,8},{8,16},{16,24},{24,32},{32,40},{40,48},{48,56},{56,64},{64,7... | collective-permute-start | bytes 6291464 | tf_op jit(solution)/shard_map/ppermute | solution.py:15
  228.6 7.7 collective-permute-start
  250.1 7.3 collective-permute-start
  269.4 7.3 collective-permute-start
  290.7 7.3 collective-permute-start
  310.0 7.3 collective-permute-start
  331.3 7.3 collective-permute-start
  350.7 7.3 collective-permute-start
  372.0 7.3 collective-permute-start
  391.3 7.3 collective-permute-start
  412.6 7.3 collective-permute-start
  431.9 7.3 collective-permute-start
  453.2 7.3 collective-permute-start
  472.5 7.3 collective-permute-start
  534.5 7.3 collective-permute-start
  553.8 7.3 collective-permute-start
  575.1 7.3 collective-permute-start
  594.4 7.3 collective-permute-start
  615.7 7.3 collective-permute-start
  635.0 7.3 collective-permute-start
  656.3 7.3 collective-permute-start
  675.7 7.3 collective-permute-start
  697.0 7.3 collective-permute-start
  716.3 7.3 collective-permute-start
  737.6 7.3 collective-permute-start
  756.9 7.3 collective-permute-start
  778.2 7.3 collective-permute-start
  797.5 7.3 collective-permute-start
  818.8 7.3 collective-permute-start
  838.2 7.3 collective-permute-start
  (8 other events, 39.3 us)
Sparse Core Ops, SparseCore 0:
  10.9 36.7 all-gather.5
  159.5 59.6 all-gather.7
where the time goes:
time: 900 us; the launch traced here: 896 us
  blocking collectives  374 us (42%)
  waiting for transfers between devices  270 us (30%)
  other arithmetic  89.1 us (10%)
  starting transfers between devices  65.8 us (7%)
  matrix products  58.9 us (7%)
  local copies, waits for them, and re-layouts  21.8 us (2%)
  between operations  15 us (2%)
    all_gather x31, blocking collectives, advance(): whole_vector = lax.all_gather(incoming, 'state', axis=0, tiled=True)  309 us
    ppermute x32, waiting for transfers between devices, from_behind(): lax.ppermute(value, axis, [(source, source + steps) for source in range(i...  198 us
    ppermute x32, starting transfers between devices, from_behind(): lax.ppermute(value, axis, [(source, source + steps) for source in range(i...  65.8 us
    all_gather x1, waiting for transfers between devices, on_device(): lax.all_gather(weights, 'state', axis=1, tiled=True)  54.5 us
    dot_general x32, matrix products, apply_cols(): jnp.dot(jnp.exp(vector - vector_top)[None, :], scaled_exp, precision=lax....  29.6 us
    reduce_max x32, other arithmetic, apply_cols(): vector_top = jnp.max(vector)  22.9 us
    exp x32, other arithmetic, apply_cols(): jnp.exp(vector - vector_top)[None, :]  22.8 us
    select_n x31, other arithmetic, advance(): return jnp.where(position < 2, start_cols, apply_cols(whole_vector))  21.7 us
  transfers between devices with their start and end apart: 34, of which 34 were waited for; matrix products, arithmetic and copies ran while one was open for 1% of the time, Pallas kernels for 0%

commit v1 on v0

v1 whole, which is shorter than its diff:
```python
import functools
import math

import jax
import jax.numpy as jnp
from jax import lax
from jax.experimental import pallas as pl
from jax.experimental.pallas import tpu as pltpu
from jax.sharding import PartitionSpec as P

SMOOTH = 0.001
MESH = pl.DeviceIdType.MESH
RISES = (5, 11, 20, 32, 46)
SPAN_MAX = 1 + len(RISES)


def span_of(group):
    span = jnp.int32(1)
    for rise in RISES:
        span = span + (group >= rise).astype(jnp.int32)
    return span


def inverse_of(value):
    def halves(x):
        scaled = x * 4097.0
        high = scaled - (scaled - x)
        return high, x - high

    quotient = 1.0 / value
    product = value * quotient
    value_high, value_low = halves(value)
    quotient_high, quotient_low = halves(quotient)
    excess = value_high * quotient_high - product
    excess = excess + value_high * quotient_low + value_low * quotient_high + value_low * quotient_low
    return quotient + quotient * ((1.0 - product) - excess)


def gather_kernel(groups, peers, obs_ref, trans_ref, emit_ref, blocks_ref, emis_ref,
                  obs_all, obs_send, obs_recv, blk_send, blk_recv, em_send, em_recv):
    group = lax.axis_index("tm")
    me = lax.axis_index("state")
    core = me % 2
    chip = me // 2
    chips = peers // 2
    sibling = me + 1 - 2 * core
    own_rows = trans_ref.shape[0]
    steps = obs_ref.shape[0]

    barrier = pltpu.get_barrier_semaphore()
    for other in range(1, peers):
        pl.semaphore_signal(barrier, inc=1, device_id=(group, (me + other) % peers), device_id_type=MESH)
    for back in range(1, SPAN_MAX):
        for target in ((group + back) % groups, (group + groups - back) % groups):
            pl.semaphore_signal(barrier, inc=1, device_id=(target, me), device_id_type=MESH)

    for row in range(own_rows):
        tiles = [trans_ref[row, k] for k in range(trans_ref.shape[1])]
        top = jnp.max(functools.reduce(jnp.maximum, tiles), axis=1, keepdims=True)
        tiles = [jnp.exp(tile - top) for tile in tiles]
        width = tiles[0].shape[1]
        totals = []
        for tile in tiles:
            for shift in (16, 32, 64, 8, 4, 2, 1):
                tile = tile + pltpu.roll(tile, width - shift, 1)
            totals.append(tile)
        inverse = inverse_of(functools.reduce(jnp.add, totals)[:, :1])
        for k, tile in enumerate(tiles):
            blocks_ref[own_rows * me + row, :, k * width:(k + 1) * width] = (
                (1.0 - SMOOTH) * (tile * inverse)).astype(jnp.bfloat16)

    pl.semaphore_wait(barrier, peers - 1 + 2 * (SPAN_MAX - 1))

    def obs_copy(back):
        return pltpu.make_async_remote_copy(
            src_ref=obs_ref, dst_ref=obs_all.at[back], send_sem=obs_send.at[back], recv_sem=obs_recv.at[back],
            device_id=((group + back) % groups, me), device_id_type=MESH)

    def block_copy(owner, target, sem):
        rows = blocks_ref.at[pl.ds(own_rows * owner, own_rows)]
        return pltpu.make_async_remote_copy(
            src_ref=rows, dst_ref=rows, send_sem=blk_send.at[sem], recv_sem=blk_recv.at[owner],
            device_id=(group, target), device_id_type=MESH)

    def emis_copy(owner, target, sem):
        part = emis_ref.at[owner]
        return pltpu.make_async_remote_copy(
            src_ref=part, dst_ref=part, send_sem=em_send.at[sem], recv_sem=em_recv.at[owner],
            device_id=(group, target), device_id_type=MESH)

    obs_copies = [obs_copy(back) for back in range(1, SPAN_MAX)]
    for copy in obs_copies:
        copy.start()
    sent = []
    for away in (2, 1, 3)[:chips - 1]:
        sent.append(block_copy(me, 2 * ((chip + away) % chips) + core, away))
        sent[-1].start()
    sent.append(block_copy(me, sibling, 0))
    sent[-1].start()

    logits = emit_ref[...]
    weights = jnp.exp(logits - jnp.max(logits, axis=0, keepdims=True))
    table = weights / jnp.sum(weights, axis=0, keepdims=True)
    obs_all[0] = obs_ref[...]
    for copy in obs_copies:
        copy.wait()
    symbols = logits.shape[0]
    seen = obs_all[...].reshape(SPAN_MAX * steps, obs_ref.shape[1])
    lane = lax.broadcasted_iota(jnp.int32, seen.shape, 1)
    onehot = jnp.concatenate(
        [(seen == lane + first).astype(jnp.float32) for first in range(0, symbols, seen.shape[1])], axis=1)
    emis_ref[me] = jnp.dot(onehot, table, precision=lax.Precision.HIGHEST, preferred_element_type=jnp.float32)
    for other in range(1, peers):
        sent.append(emis_copy(me, (me + other) % peers, other))
        sent[-1].start()

    for away in (1, 3, 2)[:chips - 1]:
        owner = 2 * ((chip + chips - away) % chips) + core
        block_copy(owner, sibling, 0).wait_recv()
        sent.append(block_copy(owner, sibling, chips + away))
        sent[-1].start()
    for away in range(chips):
        block_copy(2 * ((chip + away) % chips) + 1 - core, sibling, 0).wait_recv()
    for other in range(1, peers):
        emis_copy((me + other) % peers, sibling, 0).wait_recv()
    for copy in sent:
        copy.wait_send()


def form_kernel(band_ref, blocks_ref, emis_ref, high_ref, low_ref, gain_ref, matrix, scaled):
    group = lax.axis_index("tm")
    me = lax.axis_index("state")
    block_rows, block, cols = matrix.shape
    filled = blocks_ref.shape[2] // block
    states = block_rows * block
    log_symbols = math.log(256.0)
    steps = 8
    row_id = lax.broadcasted_iota(jnp.int32, (block, cols), 0)
    col_id = lax.broadcasted_iota(jnp.int32, (block, cols), 1)
    for r in range(block_rows):
        matrix[r] = (row_id + r * block == col_id + me * cols).astype(jnp.float32)

    def step(index, carry):
        inverse, log_scale = carry
        tile = pl.ds(pl.multiple_of((index // steps) * steps, steps), steps)
        now = lax.broadcasted_iota(jnp.int32, (steps, cols), 0) == steps - 1 - index % steps
        col_sum = jnp.zeros((8, cols), jnp.float32)
        for r in range(block_rows):
            start = r * block
            if start % cols == 0:
                row = jnp.sum(jnp.where(now, emis_ref[start // cols, tile, :], 0.0), axis=0, keepdims=True)
            column = jnp.broadcast_to(row[:, start % cols:start % cols + block], (block, block)).T
            column = jnp.concatenate([column] * (cols // block), axis=1)
            part = (column * (matrix[r] * inverse)).astype(jnp.bfloat16)
            scaled[r] = part
            col_sum = col_sum + jnp.sum(part.astype(jnp.float32).reshape(block // 8, 8, cols), axis=0)
        smooth = (SMOOTH / states) * jnp.sum(col_sum, axis=0, keepdims=True)
        peak = jnp.zeros((8, cols), jnp.float32)
        for r in range(block_rows):
            picked = jnp.concatenate([scaled[band_ref[r, k]] for k in range(filled)], axis=0)
            product = jnp.dot(blocks_ref[r], picked, preferred_element_type=jnp.float32) + smooth
            matrix[r] = product
            peak = jnp.maximum(peak, jnp.max(product.reshape(block // 8, 8, cols), axis=0))
        peak = jnp.max(peak, axis=0, keepdims=True)
        return 1.0 / peak, log_scale + (jnp.log(peak) + log_symbols)

    inverse, log_scale = lax.fori_loop(
        0, steps * span_of(group), step, (jnp.ones((1, cols), jnp.float32), jnp.zeros((1, cols), jnp.float32)))
    gain_ref[...] = jnp.exp(log_scale)
    for r in range(block_rows):
        whole = matrix[r] * inverse
        high = whole.astype(jnp.bfloat16)
        high_ref[r] = high
        low_ref[r] = (whole - high.astype(jnp.float32)).astype(jnp.bfloat16)


def chain_kernel(groups, peers, init_ref, high_ref, low_ref, gain_ref, out_ref,
                 parts, peer_parts, mine, recv, send, peer_send, peer_recv):
    group = lax.axis_index("tm")
    me = lax.axis_index("state")
    source = group - span_of(group)
    has_source = source >= 0
    feeds = [
        jnp.logical_and(group + ahead < groups, span_of(group + ahead) == ahead)
        for ahead in range(1, SPAN_MAX + 1)
    ]

    barrier = pltpu.get_barrier_semaphore()
    expected = jnp.int32(peers - 1)
    for other in range(1, peers):
        pl.semaphore_signal(barrier, inc=1, device_id=(group, (me + other) % peers), device_id_type=MESH)

    @pl.when(has_source)
    def _():
        for peer in range(peers):
            pl.semaphore_signal(barrier, inc=1, device_id=(source, peer), device_id_type=MESH)

    expected = expected + peers * has_source.astype(jnp.int32)
    for ahead, fed in enumerate(feeds, 1):
        @pl.when(fed)
        def _():
            for peer in range(peers):
                pl.semaphore_signal(barrier, inc=1, device_id=(group + ahead, peer), device_id_type=MESH)

        expected = expected + peers * fed.astype(jnp.int32)

    def onward(ahead, slot, peer):
        return pltpu.make_async_remote_copy(
            src_ref=mine, dst_ref=parts.at[slot], send_sem=send.at[ahead, peer], recv_sem=recv.at[slot],
            device_id=(group + ahead, peer), device_id_type=MESH)

    def to_peer(slot, peer, sem):
        return pltpu.make_async_remote_copy(
            src_ref=mine, dst_ref=peer_parts.at[slot], send_sem=peer_send.at[sem], recv_sem=peer_recv.at[slot],
            device_id=(group, peer), device_id_type=MESH)

    @pl.when(jnp.logical_not(has_source))
    def _():
        parts[...] = jnp.exp(init_ref[...] - jnp.max(init_ref[...]))

    @pl.when(has_source)
    def _():
        for peer in range(peers):
            onward(0, peer, 0).wait_recv()

    width = parts.shape[2]
    first_row = lax.broadcasted_iota(jnp.int32, (16, width), 0) == 0
    by_high = jnp.zeros((16, width), jnp.float32)
    by_low = jnp.zeros((16, width), jnp.float32)
    total = jnp.zeros((1, width), jnp.float32)
    depth = high_ref.shape[1]
    for peer in range(peers):
        part = parts[peer]
        total = total + part
        spread = jnp.broadcast_to(part, (16, width))
        rest = spread - spread.astype(jnp.bfloat16).astype(jnp.float32)
        both = jnp.where(first_row, spread, rest).astype(jnp.bfloat16)
        rows = slice(peer * (width // depth), (peer + 1) * (width // depth))
        by_high += jnp.dot(both, high_ref[rows].reshape(width, width), preferred_element_type=jnp.float32)
        by_low += jnp.dot(both, low_ref[rows].reshape(width, width), preferred_element_type=jnp.float32)
    norm = gain_ref[...] / jnp.sum(total, axis=1, keepdims=True)
    fresh = (by_high[0:1] + by_high[1:2] + by_low[0:1]) * norm
    mine[...] = fresh

    pl.semaphore_wait(barrier, expected)
    for ahead, fed in enumerate(feeds, 1):
        @pl.when(fed)
        def _():
            for peer in range(peers):
                onward(ahead, me, peer).start()

    for other in range(1, peers):
        to_peer(me, (me + other) % peers, other).start()
    whole = fresh
    for other in range(1, peers):
        slot = (me + other) % peers
        to_peer(slot, slot, other).wait_recv()
        whole = whole + peer_parts[slot]
    out_ref[...] = jnp.log(fresh) - jnp.log(jnp.sum(whole, axis=1, keepdims=True))
    for other in range(1, peers):
        to_peer(me, (me + other) % peers, other).wait_send()
    for ahead, fed in enumerate(feeds, 1):
        @pl.when(fed)
        def _():
            for peer in range(peers):
                onward(ahead, me, peer).wait_send()


def on_device(obs, emit_logits, trans_logits, band_cols, init_logits):
    peers = lax.axis_size("state")
    groups = lax.axis_size("tm")
    cols = emit_logits.shape[1]
    own_rows, filled, block, _ = trans_logits.shape
    block_rows = own_rows * peers
    steps = obs.shape[0]
    vmem = pl.BlockSpec(memory_space=pltpu.VMEM)
    dma = pltpu.SemaphoreType.DMA

    obs_wide = jnp.broadcast_to(obs[:, None], (steps, 128))
    blocks, emis = pl.pallas_call(
        functools.partial(gather_kernel, groups, peers),
        out_shape=(
            jax.ShapeDtypeStruct((block_rows, block, filled * block), jnp.bfloat16),
            jax.ShapeDtypeStruct((peers, SPAN_MAX * steps, cols), jnp.float32),
        ),
        in_specs=[vmem] * 3,
        out_specs=(vmem, vmem),
        scratch_shapes=[
            pltpu.VMEM((SPAN_MAX, steps, 128), jnp.int32),
            dma((SPAN_MAX,)), dma((SPAN_MAX,)),
            dma((peers,)), dma((peers,)),
            dma((peers,)), dma((peers,)),
        ],
        compiler_params=pltpu.CompilerParams(
            collective_id=0, has_side_effects=True, vmem_limit_bytes=32 * 2**20),
        name="gather",
    )(obs_wide, trans_logits, emit_logits)

    high, low, gain = pl.pallas_call(
        form_kernel,
        out_shape=(
            jax.ShapeDtypeStruct((block_rows, block, cols), jnp.bfloat16),
            jax.ShapeDtypeStruct((block_rows, block, cols), jnp.bfloat16),
            jax.ShapeDtypeStruct((1, cols), jnp.float32),
        ),
        in_specs=[pl.BlockSpec(memory_space=pltpu.SMEM), vmem, vmem],
        out_specs=(vmem, vmem, vmem),
        scratch_shapes=[
            pltpu.VMEM((block_rows, block, cols), jnp.float32),
            pltpu.VMEM((block_rows, block, cols), jnp.bfloat16),
        ],
        compiler_params=pltpu.CompilerParams(vmem_limit_bytes=40 * 2**20),
        name="form",
    )(band_cols, blocks, emis)

    return pl.pallas_call(
        functools.partial(chain_kernel, groups, peers),
        out_shape=jax.ShapeDtypeStruct((1, cols), jnp.float32),
        in_specs=[vmem] * 4,
        out_specs=vmem,
        scratch_shapes=[
            pltpu.VMEM((peers, 1, cols), jnp.float32),
            pltpu.VMEM((peers, 1, cols), jnp.float32),
            pltpu.VMEM((1, cols), jnp.float32),
            dma((peers,)), dma((SPAN_MAX + 1, peers)),
            dma((peers,)), dma((peers,)),
        ],
        compiler_params=pltpu.CompilerParams(
            collective_id=1, has_side_effects=True, vmem_limit_bytes=32 * 2**20),
        name="chain",
    )(init_logits.reshape(peers, 1, cols), high, low, gain)


def solution(mesh):
    return jax.shard_map(
        on_device,
        mesh=mesh,
        in_specs=(P("tm"), P(None, "state"), P("state", None, None, None), P(), P()),
        out_specs=P("tm", "state"),
        check_vma=False,
    )
```

time: 900 us -> 153 us (0.17)
  the two profiles are of different devices: /device:TPU:25 before, /device:TPU:505 now
where the time goes in v1:
time: 153 us; the launch traced here: 152 us
  Pallas kernels  148 us (97%)
  local copies, waits for them, and re-layouts  4.01 us (3%)
    pallas_call x1, Pallas kernels, on_device(): pl.pallas_call(functools.partial(chain_kernel, groups, peers), out_shape=...  70.7 us
    pallas_call x1, Pallas kernels, on_device(): pl.pallas_call(form_kernel, out_shape=(jax.ShapeDtypeStruct((block_rows,...  56.2 us
    pallas_call x1, Pallas kernels, on_device(): pl.pallas_call(functools.partial(gather_kernel, groups, peers), out_shape...  21.4 us
    unnamed x8, local copies, waits for them, and re-layouts  3.27 us

profile of v1, /device:TPU:505, one launch (start us, length us, event | category | flops | bytes accessed | tf_op | source)
XLA Modules:
  0.0 152.3 jit_solution(10882588397237798145)
XLA Ops:
  0.0 0.0 copy-start.2
  0.0 0.7 broadcast_in_dim.2.obs_ref
  0.7 0.8 copy.6.band_ref
  1.5 0.0 copy-start
  1.5 1.0 copy-done
  2.5 0.0 copy-start.1
  2.5 0.9 copy-done.1
  3.4 21.4 %gather.1 = (bf16[16,128,384]{2,1,0:T(8,128)(2,1)S(1)}, f32[8,48,256]{2,1,0:T(8,128)S(1)}) custom-call(s32[8,128]{1,0:T(8,128)S(1)} %broadcast_in_dim.2.obs_ref, f32[2,3,128,128]{3,2,1,0:T(8,128)S(1)} %copy-done, f32[256,256]{1,0:T(8,128)S(1)} %copy-done.1), custom_call_target="tpu_custom_call" | custom-call | tf_op jit(solution)/shard_map/gather/pallas_call | solution.py:280
  24.8 56.2 %form.1 = (bf16[16,128,256]{2,1,0:T(8,128)(2,1)S(1)}, bf16[16,128,256]{2,1,0:T(8,128)(2,1)S(1)}, f32[1,256]{1,0:T(1,128)S(1)}) custom-call(s32[16,3]{1,0:T(8,128)S(1)} %copy.6.band_ref, bf16[16,128,384]{2,1,0:T(8,128)(2,1)S(1)} %get-tuple-element.10.blocks_ref, f32[8,48,256]{2,1,0:T(8,128)S(1)} %get-tuple-element.11.emis_ref), custom_call_target="tpu_custom_call" | custom-call | tf_op jit(solution)/shard_map/form/pallas_call | solution.py:299
  81.0 0.0 copy-done.2
  81.0 70.7 %chain.1 = f32[1,256]{1,0:T(1,128)S(1)} custom-call(f32[8,1,256]{2,1,0:T(1,128)S(1)} %bitcast.1, bf16[16,128,256]{2,1,0:T(8,128)(2,1)S(1)} %get-tuple-element.12.high_ref, bf16[16,128,256]{2,1,0:T(8,128)(2,1)S(1)} %get-tuple-element.13.low_ref, f32[1,256]{1,0:T(1,128)S(1)} %get-tuple-element.14.gain_ref), custom_call_target="tpu_custom_call" | custom-call | tf_op jit(solution)/shard_map/chain/pallas_call | solution.py:316
  151.8 0.6 copy.8
Async XLA Ops:
  0.0 81.0 %copy-start.2 = (f32[2048]{0:T(1024)S(1)}, f32[2048]{0:T(1024)}, u32[]{:S(2)}) copy-start(f32[2048]{0:T(1024)} %param.9) | copy-start | bytes 24580
  1.5 1.0 copy-start
  2.5 0.9 copy-start.1

commit v2 on v1

--- a/solution.py
+++ b/solution.py
@@ -10,7 +10,8 @@
 
 SMOOTH = 0.001
 MESH = pl.DeviceIdType.MESH
-RISES = (5, 11, 20, 32, 46)
+DEEP = 16
+RISES = (4, 13, 20, 50, 53, 57)
 SPAN_MAX = 1 + len(RISES)
 
 
@@ -19,6 +20,19 @@
     for rise in RISES:
         span = span + (group >= rise).astype(jnp.int32)
     return span
+
+
+def group_at(place, groups):
+    return place % DEEP * (groups // DEEP) + place // DEEP
+
+
+def place_of(group, groups):
+    high = groups // DEEP
+    return group % high * DEEP + group // high
+
+
+def when_all(*conditions):
+    return pl.when(functools.reduce(jnp.logical_and, conditions))
 
 
 def inverse_of(value):
@@ -36,24 +50,49 @@
     return quotient + quotient * ((1.0 - product) - excess)
 
 
-def gather_kernel(groups, peers, obs_ref, trans_ref, emit_ref, blocks_ref, emis_ref,
-                  obs_all, obs_send, obs_recv, blk_send, blk_recv, em_send, em_recv):
-    group = lax.axis_index("tm")
+def gather_kernel(groups, peers, obs_ref, trans_hbm, emit_hbm, blocks_ref, emis_ref,
+                  trans_ref, emit_ref, load, obs_all, obs_send, obs_recv, blk_send, blk_recv, em_send, em_recv):
+    place = lax.axis_index("tm")
+    group = group_at(place, groups)
     me = lax.axis_index("state")
     core = me % 2
     chip = me // 2
     chips = peers // 2
     sibling = me + 1 - 2 * core
     own_rows = trans_ref.shape[0]
-    steps = obs_ref.shape[0]
+    steps = obs_all.shape[1]
+    loads = [pltpu.make_async_copy(trans_hbm, trans_ref, load.at[0]),
+             pltpu.make_async_copy(emit_hbm, emit_ref, load.at[1])]
+    for copy in loads:
+        copy.start()
+
+    def feeds(back):
+        later = place + back
+        used = jnp.logical_and(later < groups, span_of(later) > back)
+        target = place_of(later, groups)
+        return used, target, target == place
+
+    def fed_by(back):
+        used = jnp.logical_and(group >= back, span_of(group) > back)
+        origin = group - back
+        return used, origin, origin == place
 
     barrier = pltpu.get_barrier_semaphore()
     for other in range(1, peers):
-        pl.semaphore_signal(barrier, inc=1, device_id=(group, (me + other) % peers), device_id_type=MESH)
-    for back in range(1, SPAN_MAX):
-        for target in ((group + back) % groups, (group + groups - back) % groups):
-            pl.semaphore_signal(barrier, inc=1, device_id=(target, me), device_id_type=MESH)
-
+        pl.semaphore_signal(barrier, inc=1, device_id=(place, (me + other) % peers), device_id_type=MESH)
+    expected = jnp.int32(peers - 1)
+    for back in range(SPAN_MAX):
+        for side in (feeds, fed_by):
+            used, partner, same = side(back)
+            far = jnp.logical_and(used, jnp.logical_not(same))
+
+            @pl.when(far)
+            def _():
+                pl.semaphore_signal(barrier, inc=1, device_id=(partner, me), device_id_type=MESH)
+
+            expected = expected + far.astype(jnp.int32)
+
+    loads[0].wait()
     for row in range(own_rows):
         tiles = [trans_ref[row, k] for k in range(trans_ref.shape[1])]
         top = jnp.max(functools.reduce(jnp.maximum, tiles), axis=1, keepdims=True)
@@ -69,28 +108,40 @@
             blocks_ref[own_rows * me + row, :, k * width:(k + 1) * width] = (
                 (1.0 - SMOOTH) * (tile * inverse)).astype(jnp.bfloat16)
 
-    pl.semaphore_wait(barrier, peers - 1 + 2 * (SPAN_MAX - 1))
-
-    def obs_copy(back):
+    pl.semaphore_wait(barrier, expected)
+
+    def obs_copy(back, target):
         return pltpu.make_async_remote_copy(
             src_ref=obs_ref, dst_ref=obs_all.at[back], send_sem=obs_send.at[back], recv_sem=obs_recv.at[back],
-            device_id=((group + back) % groups, me), device_id_type=MESH)
+            device_id=(target, me), device_id_type=MESH)
 
     def block_copy(owner, target, sem):
         rows = blocks_ref.at[pl.ds(own_rows * owner, own_rows)]
         return pltpu.make_async_remote_copy(
             src_ref=rows, dst_ref=rows, send_sem=blk_send.at[sem], recv_sem=blk_recv.at[owner],
-            device_id=(group, target), device_id_type=MESH)
+            device_id=(place, target), device_id_type=MESH)
 
     def emis_copy(owner, target, sem):
         part = emis_ref.at[owner]
         return pltpu.make_async_remote_copy(
             src_ref=part, dst_ref=part, send_sem=em_send.at[sem], recv_sem=em_recv.at[owner],
-            device_id=(group, target), device_id_type=MESH)
-
-    obs_copies = [obs_copy(back) for back in range(1, SPAN_MAX)]
-    for copy in obs_copies:
-        copy.start()
+            device_id=(place, target), device_id_type=MESH)
+
+    for back in range(SPAN_MAX):
+        used, target, same = feeds(back)
+
+        @when_all(used, jnp.logical_not(same))
+        def _():
+            obs_copy(back, target).start()
+
+        @when_all(used, same)
+        def _():
+            obs_all[back] = obs_ref[...]
+
+        @pl.when(jnp.logical_not(fed_by(back)[0]))
+        def _():
+            obs_all[back] = jnp.zeros(obs_ref.shape, obs_ref.dtype)
+
     sent = []
     for away in (2, 1, 3)[:chips - 1]:
         sent.append(block_copy(me, 2 * ((chip + away) % chips) + core, away))
@@ -98,14 +149,19 @@
     sent.append(block_copy(me, sibling, 0))
     sent[-1].start()
 
+    loads[1].wait()
     logits = emit_ref[...]
     weights = jnp.exp(logits - jnp.max(logits, axis=0, keepdims=True))
     table = weights / jnp.sum(weights, axis=0, keepdims=True)
-    obs_all[0] = obs_ref[...]
-    for copy in obs_copies:
-        copy.wait()
+    for back in range(SPAN_MAX):
+        used, origin, same = fed_by(back)
+
+        @when_all(used, jnp.logical_not(same))
+        def _():
+            obs_copy(back, origin).wait_recv()
+
     symbols = logits.shape[0]
-    seen = obs_all[...].reshape(SPAN_MAX * steps, obs_ref.shape[1])
+    seen = obs_all[...].reshape(SPAN_MAX * steps, obs_all.shape[2])
     lane = lax.broadcasted_iota(jnp.int32, seen.shape, 1)
     onehot = jnp.concatenate(
         [(seen == lane + first).astype(jnp.float32) for first in range(0, symbols, seen.shape[1])], axis=1)
@@ -125,10 +181,16 @@
         emis_copy((me + other) % peers, sibling, 0).wait_recv()
     for copy in sent:
         copy.wait_send()
-
-
-def form_kernel(band_ref, blocks_ref, emis_ref, high_ref, low_ref, gain_ref, matrix, scaled):
-    group = lax.axis_index("tm")
+    for back in range(SPAN_MAX):
+        used, target, same = feeds(back)
+
+        @when_all(used, jnp.logical_not(same))
+        def _():
+            obs_copy(back, target).wait_send()
+
+
+def form_kernel(groups, band_hbm, blocks_ref, emis_ref, high_ref, low_ref, gain_ref, band_here, loaded, matrix, scaled):
+    group = group_at(lax.axis_index("tm"), groups)
     me = lax.axis_index("state")
     block_rows, block, cols = matrix.shape
     filled = blocks_ref.shape[2] // block
@@ -137,8 +199,12 @@
     steps = 8
     row_id = lax.broadcasted_iota(jnp.int32, (block, cols), 0)
     col_id = lax.broadcasted_iota(jnp.int32, (block, cols), 1)
+    load = pltpu.make_async_copy(band_hbm, band_here, loaded)
+    load.start()
     for r in range(block_rows):
         matrix[r] = (row_id + r * block == col_id + me * cols).astype(jnp.float32)
+
+    load.wait()
 
     def step(index, carry):
         inverse, log_scale = carry
@@ -151,13 +217,13 @@
                 row = jnp.sum(jnp.where(now, emis_ref[start // cols, tile, :], 0.0), axis=0, keepdims=True)
             column = jnp.broadcast_to(row[:, start % cols:start % cols + block], (block, block)).T
             column = jnp.concatenate([column] * (cols // block), axis=1)
-            part = (column * (matrix[r] * inverse)).astype(jnp.bfloat16)
-            scaled[r] = part
-            col_sum = col_sum + jnp.sum(part.astype(jnp.float32).reshape(block // 8, 8, cols), axis=0)
+            part = column * (matrix[r] * inverse)
+            scaled[r] = part.astype(jnp.bfloat16)
+            col_sum = col_sum + jnp.sum(part.reshape(block // 8, 8, cols), axis=0)
         smooth = (SMOOTH / states) * jnp.sum(col_sum, axis=0, keepdims=True)
         peak = jnp.zeros((8, cols), jnp.float32)
         for r in range(block_rows):
-            picked = jnp.concatenate([scaled[band_ref[r, k]] for k in range(filled)], axis=0)
+            picked = jnp.concatenate([scaled[band_here[k, r]] for k in range(filled)], axis=0)
             product = jnp.dot(blocks_ref[r], picked, preferred_element_type=jnp.float32) + smooth
             matrix[r] = product
             peak = jnp.maximum(peak, jnp.max(product.reshape(block // 8, 8, cols), axis=0))
@@ -176,7 +242,8 @@
 
 def chain_kernel(groups, peers, init_ref, high_ref, low_ref, gain_ref, out_ref,
                  parts, peer_parts, mine, recv, send, peer_send, peer_recv):
-    group = lax.axis_index("tm")
+    place = lax.axis_index("tm")
+    group = group_at(place, groups)
     me = lax.axis_index("state")
     source = group - span_of(group)
     has_source = source >= 0
@@ -188,31 +255,31 @@
     barrier = pltpu.get_barrier_semaphore()
     expected = jnp.int32(peers - 1)
     for other in range(1, peers):
-        pl.semaphore_signal(barrier, inc=1, device_id=(group, (me + other) % peers), device_id_type=MESH)
+        pl.semaphore_signal(barrier, inc=1, device_id=(place, (me + other) % peers), device_id_type=MESH)
 
     @pl.when(has_source)
     def _():
         for peer in range(peers):
-            pl.semaphore_signal(barrier, inc=1, device_id=(source, peer), device_id_type=MESH)
+            pl.semaphore_signal(barrier, inc=1, device_id=(place_of(source, groups), peer), device_id_type=MESH)
 
     expected = expected + peers * has_source.astype(jnp.int32)
     for ahead, fed in enumerate(feeds, 1):
         @pl.when(fed)
         def _():
             for peer in range(peers):
-                pl.semaphore_signal(barrier, inc=1, device_id=(group + ahead, peer), device_id_type=MESH)
+                pl.semaphore_signal(barrier, inc=1, device_id=(place_of(group + ahead, groups), peer), device_id_type=MESH)
 
         expected = expected + peers * fed.astype(jnp.int32)
 
     def onward(ahead, slot, peer):
         return pltpu.make_async_remote_copy(
             src_ref=mine, dst_ref=parts.at[slot], send_sem=send.at[ahead, peer], recv_sem=recv.at[slot],
-            device_id=(group + ahead, peer), device_id_type=MESH)
+            device_id=(place_of(group + ahead, groups), peer), device_id_type=MESH)
 
     def to_peer(slot, peer, sem):
         return pltpu.make_async_remote_copy(
             src_ref=mine, dst_ref=peer_parts.at[slot], send_sem=peer_send.at[sem], recv_sem=peer_recv.at[slot],
-            device_id=(group, peer), device_id_type=MESH)
+            device_id=(place, peer), device_id_type=MESH)
 
     @pl.when(jnp.logical_not(has_source))
     def _():
@@ -246,8 +313,8 @@
     for ahead, fed in enumerate(feeds, 1):
         @pl.when(fed)
         def _():
-            for peer in range(peers):
-                onward(ahead, me, peer).start()
+            for turn in (4, 5, 2, 3, 6, 7, 1, 0):
+                onward(ahead, me, (me - me % 2 + turn) % peers).start()
 
     for other in range(1, peers):
         to_peer(me, (me + other) % peers, other).start()
@@ -264,6 +331,29 @@
         def _():
             for peer in range(peers):
                 onward(ahead, me, peer).wait_send()
+
+
+def deliver_kernel(groups, found_ref, out_ref, send, recv):
+    place = lax.axis_index("tm")
+    me = lax.axis_index("state")
+    target = group_at(place, groups)
+    origin = place_of(place, groups)
+    moves = target != place
+    copy = pltpu.make_async_remote_copy(
+        src_ref=found_ref, dst_ref=out_ref, send_sem=send, recv_sem=recv,
+        device_id=(target, me), device_id_type=MESH)
+
+    @pl.when(moves)
+    def _():
+        barrier = pltpu.get_barrier_semaphore()
+        pl.semaphore_signal(barrier, inc=1, device_id=(origin, me), device_id_type=MESH)
+        pl.semaphore_wait(barrier, 1)
+        copy.start()
+        copy.wait()
+
+    @pl.when(jnp.logical_not(moves))
+    def _():
+        out_ref[...] = found_ref[...]
 
 
 def on_device(obs, emit_logits, trans_logits, band_cols, init_logits):
@@ -276,6 +366,7 @@
     vmem = pl.BlockSpec(memory_space=pltpu.VMEM)
     dma = pltpu.SemaphoreType.DMA
 
+    hbm = pl.BlockSpec(memory_space=pltpu.HBM)
     obs_wide = jnp.broadcast_to(obs[:, None], (steps, 128))
     blocks, emis = pl.pallas_call(
         functools.partial(gather_kernel, groups, peers),
@@ -283,9 +374,12 @@
             jax.ShapeDtypeStruct((block_rows, block, filled * block), jnp.bfloat16),
             jax.ShapeDtypeStruct((peers, SPAN_MAX * steps, cols), jnp.float32),
         ),
-        in_specs=[vmem] * 3,
+        in_specs=[vmem, hbm, hbm],
         out_specs=(vmem, vmem),
         scratch_shapes=[
+            pltpu.VMEM(trans_logits.shape, jnp.float32),
+            pltpu.VMEM(emit_logits.shape, jnp.float32),
+            dma((2,)),
             pltpu.VMEM((SPAN_MAX, steps, 128), jnp.int32),
             dma((SPAN_MAX,)), dma((SPAN_MAX,)),
             dma((peers,)), dma((peers,)),
@@ -297,23 +391,25 @@
     )(obs_wide, trans_logits, emit_logits)
 
     high, low, gain = pl.pallas_call(
-        form_kernel,
+        functools.partial(form_kernel, groups),
         out_shape=(
             jax.ShapeDtypeStruct((block_rows, block, cols), jnp.bfloat16),
             jax.ShapeDtypeStruct((block_rows, block, cols), jnp.bfloat16),
             jax.ShapeDtypeStruct((1, cols), jnp.float32),
         ),
-        in_specs=[pl.BlockSpec(memory_space=pltpu.SMEM), vmem, vmem],
+        in_specs=[hbm, vmem, vmem],
         out_specs=(vmem, vmem, vmem),
         scratch_shapes=[
+            pltpu.SMEM((filled, block_rows), jnp.int32),
+            dma,
             pltpu.VMEM((block_rows, block, cols), jnp.float32),
             pltpu.VMEM((block_rows, block, cols), jnp.bfloat16),
         ],
         compiler_params=pltpu.CompilerParams(vmem_limit_bytes=40 * 2**20),
         name="form",
-    )(band_cols, blocks, emis)
-
-    return pl.pallas_call(
+    )(band_cols.T, blocks, emis)
+
+    found = pl.pallas_call(
         functools.partial(chain_kernel, groups, peers),
         out_shape=jax.ShapeDtypeStruct((1, cols), jnp.float32),
         in_specs=[vmem] * 4,
@@ -330,6 +426,16 @@
         name="chain",
     )(init_logits.reshape(peers, 1, cols), high, low, gain)
 
+    return pl.pallas_call(
+        functools.partial(deliver_kernel, groups),
+        out_shape=jax.ShapeDtypeStruct((1, cols), jnp.float32),
+        in_specs=[vmem],
+        out_specs=vmem,
+        scratch_shapes=[dma, dma],
+        compiler_params=pltpu.CompilerParams(collective_id=2, has_side_effects=True, vmem_limit_bytes=2**20),
+        name="deliver",
+    )(found)
+
 
 def solution(mesh):
     return jax.shard_map(

time: 153 us -> 141 us (0.922)
  the two profiles are of different devices: /device:TPU:505 before, /device:TPU:488 now
where the time goes in v2:
time: 141 us; the launch traced here: 140 us
  Pallas kernels  136 us (96%)
  local copies, waits for them, and re-layouts  3.93 us (3%)
    pallas_call x1, Pallas kernels, on_device(): pl.pallas_call(functools.partial(form_kernel, groups), out_shape=(jax.Sha...  61.7 us
    pallas_call x1, Pallas kernels, on_device(): pl.pallas_call(functools.partial(chain_kernel, groups, peers), out_shape=...  34.8 us
    pallas_call x1, Pallas kernels, on_device(): pl.pallas_call(functools.partial(gather_kernel, groups, peers), out_shape...  24.5 us
    pallas_call x1, Pallas kernels, on_device(): pl.pallas_call(functools.partial(deliver_kernel, groups), out_shape=jax.S...  15.4 us
    unnamed x9, local copies, waits for them, and re-layouts  3.19 us

profile of v2, /device:TPU:488, one launch (start us, length us, event | category | flops | bytes accessed | tf_op | source)
XLA Modules:
  0.0 140.4 jit_solution(13596775601607337374)
XLA Ops:
  0.0 0.0 copy-start.2
  0.0 0.7 broadcast_in_dim.2.obs_ref
  0.7 0.0 copy-start
  0.7 1.0 copy-done
  1.7 0.0 copy-start.1
  1.7 0.9 copy-done.1
  2.7 24.5 %gather.1 = (bf16[16,128,384]{2,1,0:T(8,128)(2,1)S(1)}, f32[8,56,256]{2,1,0:T(8,128)S(1)}) custom-call(s32[8,128]{1,0:T(8,128)S(1)} %broadcast_in_dim.2.obs_ref, f32[2,3,128,128]{3,2,1,0:T(8,128)S(1)} %copy-done, f32[256,256]{1,0:T(8,128)S(1)} %copy-done.1), custom_call_target="tpu_custom_call" | custom-call | tf_op jit(solution)/shard_map/gather/pallas_call | solution.py:371
  27.2 0.0 copy-start.3
  27.2 0.7 copy-done.3
  27.9 61.7 %form.1 = (bf16[16,128,256]{2,1,0:T(8,128)(2,1)S(1)}, bf16[16,128,256]{2,1,0:T(8,128)(2,1)S(1)}, f32[1,256]{1,0:T(1,128)S(1)}) custom-call(s32[3,16]{1,0:T(4,128)S(1)} %bitcast.3, bf16[16,128,384]{2,1,0:T(8,128)(2,1)S(1)} %get-tuple-element.10.blocks_ref, f32[8,56,256]{2,1,0:T(8,128)S(1)} %get-tuple-element.11.emis_ref), custom_call_target="tpu_custom_call" | custom-call | tf_op jit(solution)/shard_map/form/pallas_call | solution.py:393
  89.6 0.0 copy-done.2
  89.6 34.8 %chain.1.found_ref = f32[1,256]{1,0:T(1,128)S(1)} custom-call(f32[8,1,256]{2,1,0:T(1,128)S(1)} %bitcast.2, bf16[16,128,256]{2,1,0:T(8,128)(2,1)S(1)} %get-tuple-element.12.high_ref, bf16[16,128,256]{2,1,0:T(8,128)(2,1)S(1)} %get-tuple-element.13.low_ref, f32[1,256]{1,0:T(1,128)S(1)} %get-tuple-element.14.gain_ref), custom_call_target="tpu_custom_call" | custom-call | tf_op jit(solution)/shard_map/chain/pallas_call | solution.py:412
  124.4 15.4 %deliver.1 = f32[1,256]{1,0:T(1,128)S(1)} custom-call(f32[1,256]{1,0:T(1,128)S(1)} %chain.1.found_ref), custom_call_target="tpu_custom_call" | custom-call | tf_op jit(solution)/shard_map/deliver/pallas_call | solution.py:429
  139.8 0.6 copy.7
Async XLA Ops:
  0.0 89.6 %copy-start.2 = (f32[2048]{0:T(1024)S(1)}, f32[2048]{0:T(1024)}, u32[]{:S(2)}) copy-start(f32[2048]{0:T(1024)} %param.9) | copy-start | bytes 24580
  0.7 1.0 copy-start
  1.7 0.9 copy-start.1
  27.2 0.7 copy-start.3

commit v3 on v2

--- a/solution.py
+++ b/solution.py
@@ -11,7 +11,7 @@
 SMOOTH = 0.001
 MESH = pl.DeviceIdType.MESH
 DEEP = 16
-RISES = (4, 13, 20, 50, 53, 57)
+RISES = (5, 9, 17, 29, 33, 45)
 SPAN_MAX = 1 + len(RISES)
 
 
@@ -23,12 +23,15 @@
 
 
 def group_at(place, groups):
-    return place % DEEP * (groups // DEEP) + place // DEEP
+    high = groups // DEEP
+    y, z = place // DEEP, place % DEEP
+    return jnp.where(z < high, y * high + z, z * high + y)
 
 
 def place_of(group, groups):
     high = groups // DEEP
-    return group % high * DEEP + group // high
+    return jnp.where(
+        group < high * high, group // high * DEEP + group % high, group % high * DEEP + group // high)
 
 
 def when_all(*conditions):
@@ -115,10 +118,10 @@
             src_ref=obs_ref, dst_ref=obs_all.at[back], send_sem=obs_send.at[back], recv_sem=obs_recv.at[back],
             device_id=(target, me), device_id_type=MESH)
 
-    def block_copy(owner, target, sem):
-        rows = blocks_ref.at[pl.ds(own_rows * owner, own_rows)]
+    def block_copy(owner, row, target, sem):
+        part = blocks_ref.at[own_rows * owner + row]
         return pltpu.make_async_remote_copy(
-            src_ref=rows, dst_ref=rows, send_sem=blk_send.at[sem], recv_sem=blk_recv.at[owner],
+            src_ref=part, dst_ref=part, send_sem=blk_send.at[sem], recv_sem=blk_recv.at[own_rows * owner + row],
             device_id=(place, target), device_id_type=MESH)
 
     def emis_copy(owner, target, sem):
@@ -143,11 +146,16 @@
             obs_all[back] = jnp.zeros(obs_ref.shape, obs_ref.dtype)
 
     sent = []
-    for away in (2, 1, 3)[:chips - 1]:
-        sent.append(block_copy(me, 2 * ((chip + away) % chips) + core, away))
+
+    def send_block(owner, row, target):
+        sent.append(block_copy(owner, row, target, len(sent)))
         sent[-1].start()
-    sent.append(block_copy(me, sibling, 0))
-    sent[-1].start()
+
+    right = 2 * ((chip + 1) % chips) + core
+    left = 2 * ((chip + chips - 1) % chips) + core
+    across = 2 * ((chip + 2) % chips) + core
+    for row, target in ((0, right), (1, left), (1, right), (0, left), (0, sibling), (1, sibling)):
+        send_block(me, row, target)
 
     loads[1].wait()
     logits = emit_ref[...]
@@ -167,20 +175,23 @@
         [(seen == lane + first).astype(jnp.float32) for first in range(0, symbols, seen.shape[1])], axis=1)
     emis_ref[me] = jnp.dot(onehot, table, precision=lax.Precision.HIGHEST, preferred_element_type=jnp.float32)
     for other in range(1, peers):
-        sent.append(emis_copy(me, (me + other) % peers, other))
-        sent[-1].start()
-
-    for away in (1, 3, 2)[:chips - 1]:
-        owner = 2 * ((chip + chips - away) % chips) + core
-        block_copy(owner, sibling, 0).wait_recv()
-        sent.append(block_copy(owner, sibling, chips + away))
-        sent[-1].start()
+        emis_copy(me, (me + other) % peers, other).start()
+
+    for owner, row, onward in ((left, 0, right), (right, 1, left), (left, 1, None), (right, 0, None),
+                               (across, 0, None), (across, 1, None)):
+        block_copy(owner, row, sibling, 0).wait_recv()
+        if onward is not None:
+            send_block(owner, row, onward)
+        send_block(owner, row, sibling)
     for away in range(chips):
-        block_copy(2 * ((chip + away) % chips) + 1 - core, sibling, 0).wait_recv()
+        for row in range(own_rows):
+            block_copy(2 * ((chip + away) % chips) + 1 - core, row, sibling, 0).wait_recv()
     for other in range(1, peers):
         emis_copy((me + other) % peers, sibling, 0).wait_recv()
     for copy in sent:
         copy.wait_send()
+    for other in range(1, peers):
+        emis_copy(me, (me + other) % peers, other).wait_send()
     for back in range(SPAN_MAX):
         used, target, same = feeds(back)
 
@@ -189,7 +200,7 @@
             obs_copy(back, target).wait_send()
 
 
-def form_kernel(groups, band_hbm, blocks_ref, emis_ref, high_ref, low_ref, gain_ref, band_here, loaded, matrix, scaled):
+def form_kernel(groups, band_hbm, blocks_ref, emis_ref, high_ref, low_ref, gain_ref, band_here, loaded, matrix, scaled, columns):
     group = group_at(lax.axis_index("tm"), groups)
     me = lax.axis_index("state")
     block_rows, block, cols = matrix.shape
@@ -204,28 +215,37 @@
     for r in range(block_rows):
         matrix[r] = (row_id + r * block == col_id + me * cols).astype(jnp.float32)
 
+    def row_at(index, owner):
+        tile = pl.ds(pl.multiple_of((index // steps) * steps, steps), steps)
+        now = lax.broadcasted_iota(jnp.int32, (steps, cols), 0) == steps - 1 - index % steps
+        return jnp.sum(jnp.where(now, emis_ref[owner, tile, :], 0.0), axis=0, keepdims=True)
+
+    def set_column(r, row):
+        start = r * block % cols
+        columns[r] = jnp.broadcast_to(row[:, start:start + block], (block, block)).T
+
+    for r in range(block_rows):
+        set_column(r, row_at(0, r * block // cols))
     load.wait()
 
     def step(index, carry):
         inverse, log_scale = carry
-        tile = pl.ds(pl.multiple_of((index // steps) * steps, steps), steps)
-        now = lax.broadcasted_iota(jnp.int32, (steps, cols), 0) == steps - 1 - index % steps
         col_sum = jnp.zeros((8, cols), jnp.float32)
         for r in range(block_rows):
-            start = r * block
-            if start % cols == 0:
-                row = jnp.sum(jnp.where(now, emis_ref[start // cols, tile, :], 0.0), axis=0, keepdims=True)
-            column = jnp.broadcast_to(row[:, start % cols:start % cols + block], (block, block)).T
-            column = jnp.concatenate([column] * (cols // block), axis=1)
+            column = jnp.concatenate([columns[r]] * (cols // block), axis=1)
             part = column * (matrix[r] * inverse)
             scaled[r] = part.astype(jnp.bfloat16)
             col_sum = col_sum + jnp.sum(part.reshape(block // 8, 8, cols), axis=0)
         smooth = (SMOOTH / states) * jnp.sum(col_sum, axis=0, keepdims=True)
         peak = jnp.zeros((8, cols), jnp.float32)
+        following = jnp.minimum(index + 1, emis_ref.shape[1] - 1)
         for r in range(block_rows):
             picked = jnp.concatenate([scaled[band_here[k, r]] for k in range(filled)], axis=0)
             product = jnp.dot(blocks_ref[r], picked, preferred_element_type=jnp.float32) + smooth
             matrix[r] = product
+            if r * block % cols == 0:
+                row = row_at(following, r * block // cols)
+            set_column(r, row)
             peak = jnp.maximum(peak, jnp.max(product.reshape(block // 8, 8, cols), axis=0))
         peak = jnp.max(peak, axis=0, keepdims=True)
         return 1.0 / peak, log_scale + (jnp.log(peak) + log_symbols)
@@ -241,7 +261,7 @@
 
 
 def chain_kernel(groups, peers, init_ref, high_ref, low_ref, gain_ref, out_ref,
-                 parts, peer_parts, mine, recv, send, peer_send, peer_recv):
+                 parts, owned, mine, recv, send, own_send, own_recv, own_local, ready):
     place = lax.axis_index("tm")
     group = group_at(place, groups)
     me = lax.axis_index("state")
@@ -251,35 +271,52 @@
         jnp.logical_and(group + ahead < groups, span_of(group + ahead) == ahead)
         for ahead in range(1, SPAN_MAX + 1)
     ]
+    origin = place_of(place, groups)
+    at_home = group == place
+    owned_later = place > group
+    owned_earlier = place < group
+    owner_first = group_at(group, groups) < group
+    owner_later = group_at(group, groups) > group
 
     barrier = pltpu.get_barrier_semaphore()
-    expected = jnp.int32(peers - 1)
-    for other in range(1, peers):
-        pl.semaphore_signal(barrier, inc=1, device_id=(place, (me + other) % peers), device_id_type=MESH)
-
-    @pl.when(has_source)
-    def _():
-        for peer in range(peers):
-            pl.semaphore_signal(barrier, inc=1, device_id=(place_of(source, groups), peer), device_id_type=MESH)
-
-    expected = expected + peers * has_source.astype(jnp.int32)
+    expected = jnp.int32(0)
+
+    def greet(condition, target):
+        @pl.when(condition)
+        def _():
+            for peer in range(peers):
+                pl.semaphore_signal(barrier, inc=1, device_id=(target, peer), device_id_type=MESH)
+
+    @pl.when(at_home)
+    def _():
+        for other in range(1, peers):
+            pl.semaphore_signal(barrier, inc=1, device_id=(place, (me + other) % peers), device_id_type=MESH)
+
+    greet(has_source, place_of(source, groups))
+    expected = expected + (peers - 1) * at_home.astype(jnp.int32) + peers * has_source.astype(jnp.int32)
     for ahead, fed in enumerate(feeds, 1):
-        @pl.when(fed)
-        def _():
-            for peer in range(peers):
-                pl.semaphore_signal(barrier, inc=1, device_id=(place_of(group + ahead, groups), peer), device_id_type=MESH)
-
+        greet(fed, place_of(group + ahead, groups))
         expected = expected + peers * fed.astype(jnp.int32)
+    greet(owned_later, origin)
+    greet(owner_later, group)
+    expected = expected + peers * (owned_earlier.astype(jnp.int32) + owner_first.astype(jnp.int32))
 
     def onward(ahead, slot, peer):
         return pltpu.make_async_remote_copy(
             src_ref=mine, dst_ref=parts.at[slot], send_sem=send.at[ahead, peer], recv_sem=recv.at[slot],
             device_id=(place_of(group + ahead, groups), peer), device_id_type=MESH)
 
-    def to_peer(slot, peer, sem):
+    def to_owner(slot, peer):
         return pltpu.make_async_remote_copy(
-            src_ref=mine, dst_ref=peer_parts.at[slot], send_sem=peer_send.at[sem], recv_sem=peer_recv.at[slot],
-            device_id=(place, peer), device_id_type=MESH)
+            src_ref=mine, dst_ref=owned.at[slot], send_sem=own_send.at[peer], recv_sem=own_recv.at[slot],
+            device_id=(group, peer), device_id_type=MESH)
+
+    pl.semaphore_wait(barrier, expected)
+
+    @pl.when(owned_earlier)
+    def _():
+        for peer in range(peers):
+            pl.semaphore_signal(ready, inc=1, device_id=(origin, peer), device_id_type=MESH)
 
     @pl.when(jnp.logical_not(has_source))
     def _():
@@ -306,54 +343,47 @@
         by_high += jnp.dot(both, high_ref[rows].reshape(width, width), preferred_element_type=jnp.float32)
         by_low += jnp.dot(both, low_ref[rows].reshape(width, width), preferred_element_type=jnp.float32)
     norm = gain_ref[...] / jnp.sum(total, axis=1, keepdims=True)
-    fresh = (by_high[0:1] + by_high[1:2] + by_low[0:1]) * norm
-    mine[...] = fresh
-
-    pl.semaphore_wait(barrier, expected)
+    mine[...] = (by_high[0:1] + by_high[1:2] + by_low[0:1]) * norm
+
     for ahead, fed in enumerate(feeds, 1):
         @pl.when(fed)
         def _():
             for turn in (4, 5, 2, 3, 6, 7, 1, 0):
                 onward(ahead, me, (me - me % 2 + turn) % peers).start()
 
-    for other in range(1, peers):
-        to_peer(me, (me + other) % peers, other).start()
-    whole = fresh
-    for other in range(1, peers):
-        slot = (me + other) % peers
-        to_peer(slot, slot, other).wait_recv()
-        whole = whole + peer_parts[slot]
-    out_ref[...] = jnp.log(fresh) - jnp.log(jnp.sum(whole, axis=1, keepdims=True))
-    for other in range(1, peers):
-        to_peer(me, (me + other) % peers, other).wait_send()
+    @pl.when(owner_later)
+    def _():
+        pl.semaphore_wait(ready, peers)
+
+    @pl.when(at_home)
+    def _():
+        pltpu.make_async_copy(mine, owned.at[me], own_local).start()
+        for other in range(1, peers):
+            to_owner(me, (me + other) % peers).start()
+        pltpu.make_async_copy(mine, owned.at[me], own_local).wait()
+        for other in range(1, peers):
+            to_owner((me + other) % peers, 0).wait_recv()
+        for other in range(1, peers):
+            to_owner(me, (me + other) % peers).wait_send()
+
+    @pl.when(jnp.logical_not(at_home))
+    def _():
+        for peer in range(peers):
+            to_owner(me, peer).start()
+        for slot in range(peers):
+            to_owner(slot, 0).wait_recv()
+        for peer in range(peers):
+            to_owner(me, peer).wait_send()
+
+    whole = jnp.zeros((1, width), jnp.float32)
+    for slot in range(peers):
+        whole = whole + owned[slot]
+    out_ref[...] = jnp.log(owned[me]) - jnp.log(jnp.sum(whole, axis=1, keepdims=True))
     for ahead, fed in enumerate(feeds, 1):
         @pl.when(fed)
         def _():
             for peer in range(peers):
                 onward(ahead, me, peer).wait_send()
-
-
-def deliver_kernel(groups, found_ref, out_ref, send, recv):
-    place = lax.axis_index("tm")
-    me = lax.axis_index("state")
-    target = group_at(place, groups)
-    origin = place_of(place, groups)
-    moves = target != place
-    copy = pltpu.make_async_remote_copy(
-        src_ref=found_ref, dst_ref=out_ref, send_sem=send, recv_sem=recv,
-        device_id=(target, me), device_id_type=MESH)
-
-    @pl.when(moves)
-    def _():
-        barrier = pltpu.get_barrier_semaphore()
-        pl.semaphore_signal(barrier, inc=1, device_id=(origin, me), device_id_type=MESH)
-        pl.semaphore_wait(barrier, 1)
-        copy.start()
-        copy.wait()
-
-    @pl.when(jnp.logical_not(moves))
-    def _():
-        out_ref[...] = found_ref[...]
 
 
 def on_device(obs, emit_logits, trans_logits, band_cols, init_logits):
@@ -382,7 +412,7 @@
             dma((2,)),
             pltpu.VMEM((SPAN_MAX, steps, 128), jnp.int32),
             dma((SPAN_MAX,)), dma((SPAN_MAX,)),
-            dma((peers,)), dma((peers,)),
+            dma((2 * peers,)), dma((block_rows,)),
             dma((peers,)), dma((peers,)),
         ],
         compiler_params=pltpu.CompilerParams(
@@ -404,12 +434,13 @@
             dma,
             pltpu.VMEM((block_rows, block, cols), jnp.float32),
             pltpu.VMEM((block_rows, block, cols), jnp.bfloat16),
+            pltpu.VMEM((block_rows, block, block), jnp.float32),
         ],
         compiler_params=pltpu.CompilerParams(vmem_limit_bytes=40 * 2**20),
         name="form",
     )(band_cols.T, blocks, emis)
 
-    found = pl.pallas_call(
+    return pl.pallas_call(
         functools.partial(chain_kernel, groups, peers),
         out_shape=jax.ShapeDtypeStruct((1, cols), jnp.float32),
         in_specs=[vmem] * 4,
@@ -419,22 +450,13 @@
             pltpu.VMEM((peers, 1, cols), jnp.float32),
             pltpu.VMEM((1, cols), jnp.float32),
             dma((peers,)), dma((SPAN_MAX + 1, peers)),
-            dma((peers,)), dma((peers,)),
+            dma((peers,)), dma((peers,)), dma,
+            pltpu.SemaphoreType.REGULAR,
         ],
         compiler_params=pltpu.CompilerParams(
             collective_id=1, has_side_effects=True, vmem_limit_bytes=32 * 2**20),
         name="chain",
     )(init_logits.reshape(peers, 1, cols), high, low, gain)
-
-    return pl.pallas_call(
-        functools.partial(deliver_kernel, groups),
-        out_shape=jax.ShapeDtypeStruct((1, cols), jnp.float32),
-        in_specs=[vmem],
-        out_specs=vmem,
-        scratch_shapes=[dma, dma],
-        compiler_params=pltpu.CompilerParams(collective_id=2, has_side_effects=True, vmem_limit_bytes=2**20),
-        name="deliver",
-    )(found)
 
 
 def solution(mesh):

time: 141 us -> 122 us (0.87)
  the two profiles are of different devices: /device:TPU:488 before, /device:TPU:25 now
where the time goes in v3:
time: 122 us; the launch traced here: 121 us
  Pallas kernels  117 us (96%)
  local copies, waits for them, and re-layouts  3.93 us (3%)
    pallas_call x1, Pallas kernels, on_device(): pl.pallas_call(functools.partial(chain_kernel, groups, peers), out_shape=...  60.6 us
    pallas_call x1, Pallas kernels, on_device(): pl.pallas_call(functools.partial(gather_kernel, groups, peers), out_shape...  31.2 us
    pallas_call x1, Pallas kernels, on_device(): pl.pallas_call(functools.partial(form_kernel, groups), out_shape=(jax.Sha...  24.8 us
    unnamed x9, local copies, waits for them, and re-layouts  3.19 us

profile of v3, /device:TPU:25, one launch (start us, length us, event | category | flops | bytes accessed | tf_op | source)
XLA Modules:
  0.0 120.7 jit_solution(18001407171908049654)
XLA Ops:
  0.0 0.0 copy-start.2
  0.0 0.7 broadcast_in_dim.2.obs_ref
  0.7 0.0 copy-start
  0.7 1.0 copy-done
  1.7 0.0 copy-start.1
  1.7 0.9 copy-done.1
  2.7 31.2 %gather.1 = (bf16[16,128,384]{2,1,0:T(8,128)(2,1)S(1)}, f32[8,56,256]{2,1,0:T(8,128)S(1)}) custom-call(s32[8,128]{1,0:T(8,128)S(1)} %broadcast_in_dim.2.obs_ref, f32[2,3,128,128]{3,2,1,0:T(8,128)S(1)} %copy-done, f32[256,256]{1,0:T(8,128)S(1)} %copy-done.1), custom_call_target="tpu_custom_call" | custom-call | tf_op jit(solution)/shard_map/gather/pallas_call | solution.py:401
  33.9 0.0 copy-start.3
  33.9 0.7 copy-done.3
  34.6 24.8 %form.1 = (bf16[16,128,256]{2,1,0:T(8,128)(2,1)S(1)}, bf16[16,128,256]{2,1,0:T(8,128)(2,1)S(1)}, f32[1,256]{1,0:T(1,128)S(1)}) custom-call(s32[3,16]{1,0:T(4,128)S(1)} %bitcast.3, bf16[16,128,384]{2,1,0:T(8,128)(2,1)S(1)} %get-tuple-element.10.blocks_ref, f32[8,56,256]{2,1,0:T(8,128)S(1)} %get-tuple-element.11.emis_ref), custom_call_target="tpu_custom_call" | custom-call | tf_op jit(solution)/shard_map/form/pallas_call | solution.py:423
  59.4 0.0 copy-done.2
  59.4 60.6 %chain.1 = f32[1,256]{1,0:T(1,128)S(1)} custom-call(f32[8,1,256]{2,1,0:T(1,128)S(1)} %bitcast.2, bf16[16,128,256]{2,1,0:T(8,128)(2,1)S(1)} %get-tuple-element.12.high_ref, bf16[16,128,256]{2,1,0:T(8,128)(2,1)S(1)} %get-tuple-element.13.low_ref, f32[1,256]{1,0:T(1,128)S(1)} %get-tuple-element.14.gain_ref), custom_call_target="tpu_custom_call" | custom-call | tf_op jit(solution)/shard_map/chain/pallas_call | solution.py:443
  120.1 0.6 copy.7
Async XLA Ops:
  0.0 59.4 %copy-start.2 = (f32[2048]{0:T(1024)S(1)}, f32[2048]{0:T(1024)}, u32[]{:S(2)}) copy-start(f32[2048]{0:T(1024)} %param.9) | copy-start | bytes 24580
  0.7 1.0 copy-start
  1.7 0.9 copy-start.1
  33.9 0.7 copy-start.3

commit v4 on v3

--- a/solution.py
+++ b/solution.py
@@ -53,8 +53,7 @@
     return quotient + quotient * ((1.0 - product) - excess)
 
 
-def gather_kernel(groups, peers, obs_ref, trans_hbm, emit_hbm, blocks_ref, emis_ref,
-                  trans_ref, emit_ref, load, obs_all, obs_send, obs_recv, blk_send, blk_recv, em_send, em_recv):
+def gather_kernel(groups, peers, obs_ref, trans_ref, emit_ref, blocks_ref, emis_ref, obs_all, obs_send, obs_recv, blk_send, blk_recv, em_send, em_recv):
     place = lax.axis_index("tm")
     group = group_at(place, groups)
     me = lax.axis_index("state")
@@ -64,10 +63,6 @@
     sibling = me + 1 - 2 * core
     own_rows = trans_ref.shape[0]
     steps = obs_all.shape[1]
-    loads = [pltpu.make_async_copy(trans_hbm, trans_ref, load.at[0]),
-             pltpu.make_async_copy(emit_hbm, emit_ref, load.at[1])]
-    for copy in loads:
-        copy.start()
 
     def feeds(back):
         later = place + back
@@ -95,7 +90,6 @@
 
             expected = expected + far.astype(jnp.int32)
 
-    loads[0].wait()
     for row in range(own_rows):
         tiles = [trans_ref[row, k] for k in range(trans_ref.shape[1])]
         top = jnp.max(functools.reduce(jnp.maximum, tiles), axis=1, keepdims=True)
@@ -157,7 +151,6 @@
     for row, target in ((0, right), (1, left), (1, right), (0, left), (0, sibling), (1, sibling)):
         send_block(me, row, target)
 
-    loads[1].wait()
     logits = emit_ref[...]
     weights = jnp.exp(logits - jnp.max(logits, axis=0, keepdims=True))
     table = weights / jnp.sum(weights, axis=0, keepdims=True)
@@ -200,7 +193,7 @@
             obs_copy(back, target).wait_send()
 
 
-def form_kernel(groups, band_hbm, blocks_ref, emis_ref, high_ref, low_ref, gain_ref, band_here, loaded, matrix, scaled, columns):
+def form_kernel(groups, band_hbm, blocks_ref, emis_ref, result_ref, gain_ref, band_here, loaded, matrix, scaled, columns):
     group = group_at(lax.axis_index("tm"), groups)
     me = lax.axis_index("state")
     block_rows, block, cols = matrix.shape
@@ -254,13 +247,10 @@
         0, steps * span_of(group), step, (jnp.ones((1, cols), jnp.float32), jnp.zeros((1, cols), jnp.float32)))
     gain_ref[...] = jnp.exp(log_scale)
     for r in range(block_rows):
-        whole = matrix[r] * inverse
-        high = whole.astype(jnp.bfloat16)
-        high_ref[r] = high
-        low_ref[r] = (whole - high.astype(jnp.float32)).astype(jnp.bfloat16)
-
-
-def chain_kernel(groups, peers, init_ref, high_ref, low_ref, gain_ref, out_ref,
+        result_ref[r] = (matrix[r] * inverse).astype(jnp.bfloat16)
+
+
+def chain_kernel(groups, peers, init_ref, matrix_ref, gain_ref, out_ref,
                  parts, owned, mine, recv, send, own_send, own_recv, own_local, ready):
     place = lax.axis_index("tm")
     group = group_at(place, groups)
@@ -329,10 +319,9 @@
 
     width = parts.shape[2]
     first_row = lax.broadcasted_iota(jnp.int32, (16, width), 0) == 0
-    by_high = jnp.zeros((16, width), jnp.float32)
-    by_low = jnp.zeros((16, width), jnp.float32)
+    mixed = jnp.zeros((16, width), jnp.float32)
     total = jnp.zeros((1, width), jnp.float32)
-    depth = high_ref.shape[1]
+    depth = matrix_ref.shape[1]
     for peer in range(peers):
         part = parts[peer]
         total = total + part
@@ -340,10 +329,9 @@
         rest = spread - spread.astype(jnp.bfloat16).astype(jnp.float32)
         both = jnp.where(first_row, spread, rest).astype(jnp.bfloat16)
         rows = slice(peer * (width // depth), (peer + 1) * (width // depth))
-        by_high += jnp.dot(both, high_ref[rows].reshape(width, width), preferred_element_type=jnp.float32)
-        by_low += jnp.dot(both, low_ref[rows].reshape(width, width), preferred_element_type=jnp.float32)
+        mixed += jnp.dot(both, matrix_ref[rows].reshape(width, width), preferred_element_type=jnp.float32)
     norm = gain_ref[...] / jnp.sum(total, axis=1, keepdims=True)
-    mine[...] = (by_high[0:1] + by_high[1:2] + by_low[0:1]) * norm
+    mine[...] = (mixed[0:1] + mixed[1:2]) * norm
 
     for ahead, fed in enumerate(feeds, 1):
         @pl.when(fed)
@@ -404,12 +392,9 @@
             jax.ShapeDtypeStruct((block_rows, block, filled * block), jnp.bfloat16),
             jax.ShapeDtypeStruct((peers, SPAN_MAX * steps, cols), jnp.float32),
         ),
-        in_specs=[vmem, hbm, hbm],
+        in_specs=[vmem] * 3,
         out_specs=(vmem, vmem),
         scratch_shapes=[
-            pltpu.VMEM(trans_logits.shape, jnp.float32),
-            pltpu.VMEM(emit_logits.shape, jnp.float32),
-            dma((2,)),
             pltpu.VMEM((SPAN_MAX, steps, 128), jnp.int32),
             dma((SPAN_MAX,)), dma((SPAN_MAX,)),
             dma((2 * peers,)), dma((block_rows,)),
@@ -420,15 +405,14 @@
         name="gather",
     )(obs_wide, trans_logits, emit_logits)
 
-    high, low, gain = pl.pallas_call(
+    matrix, gain = pl.pallas_call(
         functools.partial(form_kernel, groups),
         out_shape=(
-            jax.ShapeDtypeStruct((block_rows, block, cols), jnp.bfloat16),
             jax.ShapeDtypeStruct((block_rows, block, cols), jnp.bfloat16),
             jax.ShapeDtypeStruct((1, cols), jnp.float32),
         ),
         in_specs=[hbm, vmem, vmem],
-        out_specs=(vmem, vmem, vmem),
+        out_specs=(vmem, vmem),
         scratch_shapes=[
             pltpu.SMEM((filled, block_rows), jnp.int32),
             dma,
@@ -443,7 +427,7 @@
     return pl.pallas_call(
         functools.partial(chain_kernel, groups, peers),
         out_shape=jax.ShapeDtypeStruct((1, cols), jnp.float32),
-        in_specs=[vmem] * 4,
+        in_specs=[vmem] * 3,
         out_specs=vmem,
         scratch_shapes=[
             pltpu.VMEM((peers, 1, cols), jnp.float32),
@@ -456,7 +440,7 @@
         compiler_params=pltpu.CompilerParams(
             collective_id=1, has_side_effects=True, vmem_limit_bytes=32 * 2**20),
         name="chain",
-    )(init_logits.reshape(peers, 1, cols), high, low, gain)
+    )(init_logits.reshape(peers, 1, cols), matrix, gain)
 
 
 def solution(mesh):

time: 122 us -> 121 us (level)
  Pallas kernels: 117 us -> 115 us
where the time goes in v4:
time: 121 us; the launch traced here: 119 us
  Pallas kernels  115 us (95%)
  local copies, waits for them, and re-layouts  3.93 us (3%)
    pallas_call x1, Pallas kernels, on_device(): pl.pallas_call(functools.partial(chain_kernel, groups, peers), out_shape=...  59.6 us
    pallas_call x1, Pallas kernels, on_device(): pl.pallas_call(functools.partial(gather_kernel, groups, peers), out_shape...  31 us
    pallas_call x1, Pallas kernels, on_device(): pl.pallas_call(functools.partial(form_kernel, groups), out_shape=(jax.Sha...  24.6 us
    unnamed x9, local copies, waits for them, and re-layouts  3.19 us

profile of v4, /device:TPU:25, one launch (start us, length us, event | category | flops | bytes accessed | tf_op | source)
XLA Modules:
  0.0 119.1 jit_solution(7191636462761578030)
XLA Ops:
  0.0 0.0 copy-start.2
  0.0 0.7 broadcast_in_dim.2.obs_ref
  0.7 0.0 copy-start
  0.7 1.0 copy-done
  1.7 0.0 copy-start.1
  1.7 0.9 copy-done.1
  2.7 31.0 %gather.1 = (bf16[16,128,384]{2,1,0:T(8,128)(2,1)S(1)}, f32[8,56,256]{2,1,0:T(8,128)S(1)}) custom-call(s32[8,128]{1,0:T(8,128)S(1)} %broadcast_in_dim.2.obs_ref, f32[2,3,128,128]{3,2,1,0:T(8,128)S(1)} %copy-done, f32[256,256]{1,0:T(8,128)S(1)} %copy-done.1), custom_call_target="tpu_custom_call" | custom-call | tf_op jit(solution)/shard_map/gather/pallas_call | solution.py:389
  33.7 0.0 copy-start.3
  33.7 0.7 copy-done.3
  34.4 24.6 %form.1 = (bf16[16,128,256]{2,1,0:T(8,128)(2,1)S(1)}, f32[1,256]{1,0:T(1,128)S(1)}) custom-call(s32[3,16]{1,0:T(4,128)S(1)} %bitcast.3, bf16[16,128,384]{2,1,0:T(8,128)(2,1)S(1)} %get-tuple-element.9.blocks_ref, f32[8,56,256]{2,1,0:T(8,128)S(1)} %get-tuple-element.10.emis_ref), custom_call_target="tpu_custom_call" | custom-call | tf_op jit(solution)/shard_map/form/pallas_call | solution.py:408
  59.0 0.0 copy-done.2
  59.0 59.6 %chain.1 = f32[1,256]{1,0:T(1,128)S(1)} custom-call(f32[8,1,256]{2,1,0:T(1,128)S(1)} %bitcast.2, bf16[16,128,256]{2,1,0:T(8,128)(2,1)S(1)} %get-tuple-element.11.matrix_ref, f32[1,256]{1,0:T(1,128)S(1)} %get-tuple-element.12.gain_ref), custom_call_target="tpu_custom_call" | custom-call | tf_op jit(solution)/shard_map/chain/pallas_call | solution.py:427
  118.6 0.6 copy.7
Async XLA Ops:
  0.0 59.0 %copy-start.2 = (f32[2048]{0:T(1024)S(1)}, f32[2048]{0:T(1024)}, u32[]{:S(2)}) copy-start(f32[2048]{0:T(1024)} %param.9) | copy-start | bytes 24580
  0.7 1.0 copy-start
  1.7 0.9 copy-start.1
  33.7 0.7 copy-start.3
